TPU v7x, 32 devices: a whole 2x2x4 slice. The times are simulated.
32 devices in a mesh: rep: 4 (over x, core), row: 4 (over z), col: 2 (over y).
Axes of the slice: x: 2, y: 2, z: 4, core: 2. Of those that a mesh axis runs over, the one named last changes fastest.
Arguments:
- inputs: bfloat16 [4, 128, 6144], P('rep', 'col', 'row'), may hold values from -6 to 6
- w_in: bfloat16 [6144, 24576], P('row', ('rep', 'col')), may hold values from -0.078125 to 0.078125
- w_out: bfloat16 [24576, 6144], P(('rep', 'col'), 'row'), may hold values from -0.0390625 to 0.0390625
- cotangent: bfloat16 [4, 128, 6144], P('rep', 'col', 'row'), may hold values from -1536 to 1536
- counts: int32 [4], replicated, may hold values from 0 to 4, as said below
Outputs:
- block_output: bfloat16 [4, 128, 6144], P('rep', 'col', 'row')
- input_grad: bfloat16 [4, 128, 6144], P('rep', 'col', 'row')
- w_in_grad: float32 [6144, 24576], P('row', ('rep', 'col'))
- w_out_grad: float32 [24576, 6144], P(('rep', 'col'), 'row')
Inputs may be any that keep to these rules, and one draw needn't show every extreme that they name: Replica r completed its first counts[r] micro-batches; at least one replica completed all 4.
All inputs are finite; a program needn't handle non-finite values.
Results may differ from a plain program's by a relative error of at most 0.015.
Values may be sent and summed in bfloat16 or wider, within the bound.
A program may use at most 192 MiB of HBM per device.

v0:
```python
import jax
import jax.numpy as jnp
from jax import lax
from jax.sharding import PartitionSpec as P

MBT = 32
root_coef = 0.7978845608028654
cubic_coef = 0.044715


def gelu_tanh(values):
    inner = root_coef * (values + cubic_coef * values * values * values)
    return 0.5 * values * (1.0 + jnp.tanh(inner))


def gelu_slope(values):
    inner = root_coef * (values + cubic_coef * values * values * values)
    tangent = jnp.tanh(inner)
    return 0.5 * (1.0 + tangent) + 0.5 * values * (1.0 - tangent * tangent) * root_coef * (
        1.0 + 3.0 * cubic_coef * values * values
    )


def right_product(left, right):
    return lax.dot_general(
        left, right, (((1,), (1,)), ((), ())), preferred_element_type=jnp.float32
    )


def first_product(left, right):
    return lax.dot_general(
        left, right, (((0,), (0,)), ((), ())), preferred_element_type=jnp.float32
    )


def body(inputs, w_in, w_out, cotangent, counts):
    rows_local = inputs.shape[1]
    width_local = inputs.shape[2]
    tokens_local = inputs.reshape(rows_local, width_local)
    replicas = lax.axis_size("rep")
    replica_index = lax.axis_index("rep")
    column_index = lax.axis_index("col")
    own_count = jnp.sum(jnp.where(jnp.arange(replicas) == replica_index, counts, 0))
    token_total = (MBT * jnp.sum(counts)).astype(jnp.float32)
    positions = column_index * rows_local + jnp.arange(rows_local, dtype=jnp.int32)
    kept_mask = (positions // MBT < own_count).astype(jnp.float32)
    scaled = (
        cotangent.reshape(rows_local, width_local).astype(jnp.float32)
        * kept_mask[:, None]
        / token_total
    ).astype(jnp.bfloat16)
    tokens_all = lax.all_gather(tokens_local, ("rep", "col"), axis=0, tiled=True)
    scaled_all = lax.all_gather(scaled, ("rep", "col"), axis=0, tiled=True)
    partial_hidden = jnp.dot(tokens_all, w_in, preferred_element_type=jnp.float32)
    hidden = lax.psum_scatter(
        partial_hidden.astype(jnp.bfloat16), "row", scatter_dimension=0, tiled=True
    ).astype(jnp.float32)
    slope_terms = right_product(scaled_all, w_out)
    slope_sum = lax.psum_scatter(
        slope_terms.astype(jnp.bfloat16), "row", scatter_dimension=0, tiled=True
    ).astype(jnp.float32)
    active_share = gelu_tanh(hidden).astype(jnp.bfloat16)
    activated = lax.all_gather(active_share, "row", axis=0, tiled=True)
    grad_share = (slope_sum * gelu_slope(hidden)).astype(jnp.bfloat16)
    hidden_grad = lax.all_gather(grad_share, "row", axis=0, tiled=True)
    output_terms = jnp.dot(activated, w_out, preferred_element_type=jnp.float32)
    output_local = lax.psum_scatter(
        output_terms.astype(jnp.bfloat16), ("rep", "col"), scatter_dimension=0, tiled=True
    ).astype(jnp.float32)
    block_output = (tokens_local.astype(jnp.float32) + output_local).astype(jnp.bfloat16)
    w_out_grad = first_product(activated, scaled_all)
    back_terms = right_product(hidden_grad, w_in)
    back_local = lax.psum_scatter(
        back_terms.astype(jnp.bfloat16), ("rep", "col"), scatter_dimension=0, tiled=True
    ).astype(jnp.float32)
    input_grad = (scaled.astype(jnp.float32) + back_local).astype(jnp.bfloat16)
    w_in_grad = first_product(tokens_all, hidden_grad)
    return (
        block_output.reshape(1, rows_local, width_local),
        input_grad.reshape(1, rows_local, width_local),
        w_in_grad,
        w_out_grad,
    )


def solution(mesh):
    placed = (
        P("rep", "col", "row"),
        P("row", ("rep", "col")),
        P(("rep", "col"), "row"),
        P("rep", "col", "row"),
        P(),
    )
    return jax.shard_map(
        body,
        mesh=mesh,
        in_specs=placed,
        out_specs=(
            P("rep", "col", "row"),
            P("rep", "col", "row"),
            P("row", ("rep", "col")),
            P(("rep", "col"), "row"),
        ),
        check_vma=False,
    )
```

profile of v0, /device:TPU:0, one launch (start us, length us, event | category | flops | bytes accessed | tf_op | source)
XLA Modules:
  0.0 415.8 jit_solution(2729077798957875447)
XLA Ops:
  7.2 0.0 all-gather.8.cloned.1.call-start
  7.2 1.3 fusion.18
  9.2 0.7 compare_convert_fusion
  9.8 1.7 fusion.14
  11.6 0.0 all-gather.8.cloned.1.call-update
  11.6 0.0 all-gather.12.cloned.1.call-start
  11.6 0.7 all-gather.12.cloned.1.call-update
  12.3 0.0 reduce-scatter.9.cloned.1.call-start
  12.4 27.6 %all-gather.8.cloned.1.call-done = bf16[512,1536]{1,0:T(8,128)(2,1)} async-done(((bf16[64,1536]{1,0:T(8,128)(2,1)}), bf16[512,1536]{1,0:T(8,128)(2,1)}) %all-gather.8.cloned.1.call-update) | async-done | bytes 1572880 | tf_op jit(solution)/shard_map/all_gather | solution.py:53
  40.0 9.3 %convolution_convert_fusion = bf16[512,3072]{1,0:T(8,128)(2,1)} fusion(bf16[512,1536]{1,0:T(8,128)(2,1)} %all-gather.8.cloned.1.call-done, bf16[3072,1536]{1,0:T(8,128)(2,1)} %param.7), kind=kOutput, calls=%fused_computation.1 | convolution fusion | flops 4833411072 | bytes 14155776 | tf_op jit(solution)/shard_map/dot_general | solution.py:25
  49.3 0.0 reduce-scatter.9.cloned.1.call-update
  49.3 0.0 reduce-scatter.5.cloned.1.call-start
  49.4 18.1 %all-gather.12.cloned.1.call-done = bf16[1,512,1536]{2,1,0:T(8,128)(2,1)} async-done(((bf16[1,64,1536]{2,1,0:T(8,128)(2,1)}), bf16[1,512,1536]{2,1,0:T(8,128)(2,1)}) %all-gather.12.cloned.1.call-update) | async-done | bytes 1572880 | tf_op jit(solution)/shard_map/all_gather | solution.py:52
  67.5 9.2 %convolution_convert_fusion.1 = bf16[512,3072]{1,0:T(8,128)(2,1)} fusion(bf16[1536,3072]{1,0:T(8,128)(2,1)} %param.6, bf16[1,512,1536]{2,1,0:T(8,128)(2,1)} %all-gather.12.cloned.1.call-done), kind=kOutput, calls=%fused_computation.2 | convolution fusion | flops 4833411072 | bytes 14155776 | tf_op jit(solution)/shard_map/dot_general | solution.py:54
  76.7 0.0 reduce-scatter.5.cloned.1.call-update
  76.7 0.0 all-gather.6.cloned.1.call-start
  76.8 54.0 %reduce-scatter.9.cloned.1.call-done = bf16[128,3072]{1,0:T(8,128)(2,1)} async-done(((bf16[512,3072]{1,0:T(8,128)(2,1)}), bf16[128,3072]{1,0:T(8,128)(2,1)}) %reduce-scatter.9.cloned.1.call-update) | async-done | bytes 786448 | tf_op jit(solution)/shard_map/reduce_scatter | solution.py:59
  130.8 63.1 %reduce-scatter.5.cloned.1.call-done = bf16[128,3072]{1,0:T(8,128)(2,1)} async-done(((bf16[512,3072]{1,0:T(8,128)(2,1)}), bf16[128,3072]{1,0:T(8,128)(2,1)}) %reduce-scatter.5.cloned.1.call-update) | async-done | bytes 786448 | tf_op jit(solution)/shard_map/reduce_scatter | solution.py:55
  193.9 3.7 fusion.7
  197.6 0.0 all-gather.6.cloned.1.call-update
  197.6 0.0 all-gather.10.cloned.1.call-start
  197.7 0.5 all-gather.10.cloned.1.call-update
  198.2 0.0 reduce-scatter.7.cloned.1.call-start
  198.2 62.9 %all-gather.6.cloned.1.call-done = bf16[512,3072]{1,0:T(8,128)(2,1)} async-done(((bf16[128,3072]{1,0:T(8,128)(2,1)}), bf16[512,3072]{1,0:T(8,128)(2,1)}) %all-gather.6.cloned.1.call-update) | async-done | bytes 3145744 | tf_op jit(solution)/shard_map/all_gather | solution.py:63
  261.1 10.3 %convolution_convert_fusion.3 = bf16[512,1536]{1,0:T(8,128)(2,1)} fusion(bf16[512,3072]{1,0:T(8,128)(2,1)} %all-gather.6.cloned.1.call-done, bf16[3072,1536]{1,0:T(8,128)(2,1)} %param.7), kind=kOutput, calls=%fused_computation.11 | convolution fusion | flops 4832624640 | bytes 14155776 | tf_op jit(solution)/shard_map/dot_general | solution.py:66
  271.4 0.0 reduce-scatter.7.cloned.1.call-update
  271.4 0.2 reduce-scatter.11.cloned.1.call-start
  271.6 53.6 %all-gather.10.cloned.1.call-done = bf16[512,3072]{1,0:T(8,128)(2,1)} async-done(((bf16[128,3072]{1,0:T(8,128)(2,1)}), bf16[512,3072]{1,0:T(8,128)(2,1)}) %all-gather.10.cloned.1.call-update) | async-done | bytes 3145744 | tf_op jit(solution)/shard_map/all_gather | solution.py:65
  325.2 0.0 copy-start.3
  325.2 10.5 %convolution_convert_fusion.2 = bf16[512,1536]{1,0:T(8,128)(2,1)} fusion(bf16[512,3072]{1,0:T(8,128)(2,1)} %all-gather.10.cloned.1.call-done, bf16[1536,3072]{1,0:T(8,128)(2,1)} %param.6), kind=kOutput, calls=%fused_computation.10 | convolution fusion | flops 4832624640 | bytes 14155776 | tf_op jit(solution)/shard_map/dot_general | solution.py:25
  335.7 0.0 reduce-scatter.11.cloned.1.call-update
  335.7 0.0 copy-done.3
  335.7 11.0 %convolution_bitcast_fusion = f32[1536,3072]{0,1:T(8,128)} fusion(bf16[512,3072]{1,0:T(8,128)(2,1)S(1)} %copy-done.3, bf16[1,512,1536]{2,1,0:T(8,128)(2,1)} %all-gather.12.cloned.1.call-done), kind=kOutput, calls=%fused_computation | convolution fusion | flops 4831838208 | bytes 23592960 | tf_op jit(solution)/shard_map/dot_general | solution.py:31
  346.8 0.0 copy-start.2
  346.8 19.0 %copy.9 = f32[1536,3072]{1,0:T(8,128)} copy(f32[1536,3072]{0,1:T(8,128)} %convolution_bitcast_fusion) | data formatting | bytes 37748736
  365.8 0.0 copy-done.2
  365.8 0.0 copy-start
  365.8 0.0 copy-start.1
  365.8 11.0 %fusion.19 = f32[3072,1536]{1,0:T(8,128)} fusion(bf16[512,3072]{1,0:T(8,128)(2,1)S(1)} %copy-done.2, bf16[512,1536]{1,0:T(8,128)(2,1)} %all-gather.8.cloned.1.call-done), kind=kOutput, calls=%fused_computation.40 | convolution fusion | flops 4831838208 | bytes 23592960 | tf_op jit(solution)/shard_map/dot_general | solution.py:31
  376.8 0.0 reduce-scatter.7.cloned.1.call-done
  376.8 0.0 copy-done
  376.8 1.7 fusion.17
  378.4 28.8 %reduce-scatter.11.cloned.1.call-done = bf16[64,1536]{1,0:T(8,128)(2,1)} async-done(((bf16[512,1536]{1,0:T(8,128)(2,1)}), bf16[64,1536]{1,0:T(8,128)(2,1)}) %reduce-scatter.11.cloned.1.call-update) | async-done | bytes 196624 | tf_op jit(solution)/shard_map/reduce_scatter | solution.py:73
  407.2 0.0 copy-done.1
  407.2 1.7 fusion.16
Async XLA Ops:
  7.2 32.9 %all-gather.8.cloned.1.call-start = ((), (), s32[]{:S(2)}) async-start(), calls=%async_computation.7 | async-start | bytes 1769472 | tf_op jit(solution)/shard_map/all_gather | solution.py:53
  11.6 55.9 %all-gather.12.cloned.1.call-start = ((), (), s32[]{:S(2)}) async-start(), calls=%async_computation.11 | async-start | bytes 1769472 | tf_op jit(solution)/shard_map/all_gather | solution.py:52
  12.3 118.5 %reduce-scatter.9.cloned.1.call-start = ((), (), s32[]{:S(2)}) async-start(), calls=%async_computation.8 | async-start | bytes 3932160 | tf_op jit(solution)/shard_map/reduce_scatter | solution.py:59
  49.3 144.6 %reduce-scatter.5.cloned.1.call-start = ((), (), s32[]{:S(2)}) async-start(), calls=%async_computation.4 | async-start | bytes 3932160 | tf_op jit(solution)/shard_map/reduce_scatter | solution.py:55
  76.7 184.4 %all-gather.6.cloned.1.call-start = ((), (), s32[]{:S(2)}) async-start(), calls=%async_computation.5 | async-start | bytes 3932160 | tf_op jit(solution)/shard_map/all_gather | solution.py:63
  197.6 127.6 %all-gather.10.cloned.1.call-start = ((), (), s32[]{:S(2)}) async-start(), calls=%async_computation.9 | async-start | bytes 3932160 | tf_op jit(solution)/shard_map/all_gather | solution.py:65
  198.2 178.6 %reduce-scatter.7.cloned.1.call-start = ((), (), s32[]{:S(2)}) async-start(), calls=%async_computation.6 | async-start | bytes 1769472 | tf_op jit(solution)/shard_map/reduce_scatter | solution.py:67
  271.4 135.8 %reduce-scatter.11.cloned.1.call-start = ((), (), s32[]{:S(2)}) async-start(), calls=%async_computation.10 | async-start | bytes 1769472 | tf_op jit(solution)/shard_map/reduce_scatter | solution.py:73
  325.2 10.5 %copy-start.3 = (bf16[512,3072]{1,0:T(8,128)(2,1)S(1)}, bf16[512,3072]{1,0:T(8,128)(2,1)}, u32[]{:S(2)}) copy-start(bf16[512,3072]{1,0:T(8,128)(2,1)} %all-gather.10.cloned.1.call-done) | copy-start | bytes 9437188
  346.8 19.0 %copy-start.2 = (bf16[512,3072]{1,0:T(8,128)(2,1)S(1)}, bf16[512,3072]{1,0:T(8,128)(2,1)}, u32[]{:S(2)}) copy-start(bf16[512,3072]{1,0:T(8,128)(2,1)} %all-gather.6.cloned.1.call-done) | copy-start | bytes 9437188
  365.8 11.0 %copy-start = (bf16[1,64,1536]{2,1,0:T(8,128)(2,1)S(1)}, bf16[1,64,1536]{2,1,0:T(8,128)(2,1)}, u32[]{:S(2)}) copy-start(bf16[1,64,1536]{2,1,0:T(8,128)(2,1)} %param.5) | copy-start | bytes 589828
  365.8 41.4 %copy-start.1 = (bf16[1,64,1536]{2,1,0:T(8,128)(2,1)S(1)}, bf16[1,64,1536]{2,1,0:T(8,128)(2,1)}, u32[]{:S(2)}) copy-start(bf16[1,64,1536]{2,1,0:T(8,128)(2,1)} %param.8) | copy-start | bytes 589828
Sparse Core Ops, SparseCore 0:
  11.7 28.2 all-gather.7
  41.9 25.5 all-gather.11
  70.4 60.3 reduce-scatter.8
  133.5 60.3 reduce-scatter.4
  197.7 63.3 all-gather.5
  263.1 62.0 all-gather.9
  328.5 36.9 reduce-scatter.6
  368.8 38.3 reduce-scatter.10
where the time goes:
time: 416 us
  waiting for transfers between devices  309 us (74%)
  matrix products  61.2 us (15%)
  local copies, waits for them, and re-layouts  19 us (5%)
  between operations  14.8 us (4%)
  other arithmetic  10.8 us (3%)
    reduce_scatter x1, waiting for transfers between devices, body(): lax.psum_scatter(partial_hidden.astype(jnp.bfloat16), 'row', scatter_dime...  63.1 us
    all_gather x1, waiting for transfers between devices, body(): activated = lax.all_gather(active_share, 'row', axis=0, tiled=True)  62.9 us
    reduce_scatter x1, waiting for transfers between devices, body(): lax.psum_scatter(slope_terms.astype(jnp.bfloat16), 'row', scatter_dimensi...  54 us
    all_gather x1, waiting for transfers between devices, body(): hidden_grad = lax.all_gather(grad_share, 'row', axis=0, tiled=True)  53.6 us
    reduce_scatter x1, waiting for transfers between devices, body(): lax.psum_scatter(back_terms.astype(jnp.bfloat16), ('rep', 'col'), scatter...  28.8 us
    all_gather x1, waiting for transfers between devices, body(): scaled_all = lax.all_gather(scaled, ('rep', 'col'), axis=0, tiled=True)  27.6 us
    dot_general x2, matrix products, first_product(): lax.dot_general(left, right, (((0,), (0,)), ((), ())), preferred_element_...  22 us
    dot_general x2, matrix products, right_product(): lax.dot_general(left, right, (((1,), (1,)), ((), ())), preferred_element_...  19.7 us
  transfers between devices with their start and end apart: 8, of which 7 were waited for; matrix products, arithmetic and copies ran while one was open for 20% of the time, Pallas kernels for 0%

commit v1 on v0

--- a/solution.py
+++ b/solution.py
@@ -60,9 +60,14 @@
         slope_terms.astype(jnp.bfloat16), "row", scatter_dimension=0, tiled=True
     ).astype(jnp.float32)
     active_share = gelu_tanh(hidden).astype(jnp.bfloat16)
-    activated = lax.all_gather(active_share, "row", axis=0, tiled=True)
     grad_share = (slope_sum * gelu_slope(hidden)).astype(jnp.bfloat16)
-    hidden_grad = lax.all_gather(grad_share, "row", axis=0, tiled=True)
+    activated, hidden_grad = jnp.split(
+        lax.all_gather(
+            jnp.concatenate([active_share, grad_share], axis=1), "row", axis=0, tiled=True
+        ),
+        [active_share.shape[1]],
+        axis=1,
+    )
     output_terms = jnp.dot(activated, w_out, preferred_element_type=jnp.float32)
     output_local = lax.psum_scatter(
         output_terms.astype(jnp.bfloat16), ("rep", "col"), scatter_dimension=0, tiled=True

time: 416 us -> 410 us (0.986)
  waiting for transfers between devices: 309 us -> 301 us
    reduce_scatter x1, waiting for transfers between devices: 63.1 us -> 54 us  [body(): lax.psum_scatter(partial_hidden.astype(jnp.bfloat16), 'row', scatter_dime...]
    reduce_scatter x1, waiting for transfers between devices: 54 us -> 63.1 us  [body(): lax.psum_scatter(slope_terms.astype(jnp.bfloat16), 'row', scatter_dimensi...]
    all_gather x1, waiting for transfers between devices: 27.6 us -> 18.8 us  [body(): scaled_all = lax.all_gather(scaled, ('rep', 'col'), axis=0, tiled=True)]
    all_gather x1, waiting for transfers between devices: 18.1 us -> 25.8 us  [body(): lax.all_gather(tokens_local, ('rep', 'col'), axis=0, tiled=True)]
    reduce_scatter x1, waiting for transfers between devices: 28.8 us -> 22.9 us  [body(): lax.psum_scatter(back_terms.astype(jnp.bfloat16), ('rep', 'col'), scatter...]
    all_gather x2 -> x1, waiting for transfers between devices: 116 us -> 115 us  [body(): lax.all_gather(jnp.concatenate([active_share, grad_share], axis=1), 'row'...]
  transfers between devices with their start and end apart: 8 -> 7, of which waited for: 7 -> 6; matrix products, arithmetic and copies ran while one was open for 20% -> 19% of each run, Pallas kernels for 0% -> 0%
where the time goes in v1:
time: 410 us; the launch traced here: 409 us
  waiting for transfers between devices  301 us (73%)
  matrix products  62.1 us (15%)
  local copies, waits for them, and re-layouts  20.2 us (5%)
  between operations  14.8 us (4%)
  other arithmetic  10.9 us (3%)
    all_gather x1, waiting for transfers between devices, body(): lax.all_gather(jnp.concatenate([active_share, grad_share], axis=1), 'row'...  115 us
    reduce_scatter x1, waiting for transfers between devices, body(): lax.psum_scatter(slope_terms.astype(jnp.bfloat16), 'row', scatter_dimensi...  63.1 us
    reduce_scatter x1, waiting for transfers between devices, body(): lax.psum_scatter(partial_hidden.astype(jnp.bfloat16), 'row', scatter_dime...  54 us
    all_gather x1, waiting for transfers between devices, body(): lax.all_gather(tokens_local, ('rep', 'col'), axis=0, tiled=True)  25.8 us
    dot_general x2, matrix products, first_product(): lax.dot_general(left, right, (((0,), (0,)), ((), ())), preferred_element_...  22.9 us
    reduce_scatter x1, waiting for transfers between devices, body(): lax.psum_scatter(back_terms.astype(jnp.bfloat16), ('rep', 'col'), scatter...  22.9 us
    unnamed x9, local copies, waits for them, and re-layouts  20.2 us
    dot_general x2, matrix products, right_product(): lax.dot_general(left, right, (((1,), (1,)), ((), ())), preferred_element_...  19.8 us
  transfers between devices with their start and end apart: 7, of which 6 were waited for; matrix products, arithmetic and copies ran while one was open for 19% of the time, Pallas kernels for 0%

profile of v1, /device:TPU:0, one launch (start us, length us, event | category | flops | bytes accessed | tf_op | source)
XLA Modules:
  0.0 409.1 jit_solution(6648753767707842027)
XLA Ops:
  7.2 0.0 all-gather.9.cloned.1.call-start
  7.2 0.7 all-gather.9.cloned.1.call-update
  7.9 0.0 all-gather.5.cloned.1.call-start
  8.0 1.3 fusion.23
  9.9 0.7 compare_convert_fusion
  10.6 1.7 fusion.19
  12.3 0.0 all-gather.5.cloned.1.call-update
  12.3 0.0 reduce-scatter.5.cloned.1.call-start
  12.4 25.8 %all-gather.9.cloned.1.call-done = bf16[1,512,1536]{2,1,0:T(8,128)(2,1)} async-done(((bf16[1,64,1536]{2,1,0:T(8,128)(2,1)}), bf16[1,512,1536]{2,1,0:T(8,128)(2,1)}) %all-gather.9.cloned.1.call-update) | async-done | bytes 1572880 | tf_op jit(solution)/shard_map/all_gather | solution.py:52
  38.2 9.2 %convolution_convert_fusion.1 = bf16[512,3072]{1,0:T(8,128)(2,1)} fusion(bf16[1536,3072]{1,0:T(8,128)(2,1)} %param.6, bf16[1,512,1536]{2,1,0:T(8,128)(2,1)} %all-gather.9.cloned.1.call-done), kind=kOutput, calls=%fused_computation.2 | convolution fusion | flops 4833411072 | bytes 14155776 | tf_op jit(solution)/shard_map/dot_general | solution.py:54
  47.4 0.0 reduce-scatter.5.cloned.1.call-update
  47.4 0.0 reduce-scatter.7.cloned.1.call-start
  47.5 18.8 %all-gather.5.cloned.1.call-done = bf16[512,1536]{1,0:T(8,128)(2,1)} async-done(((bf16[64,1536]{1,0:T(8,128)(2,1)}), bf16[512,1536]{1,0:T(8,128)(2,1)}) %all-gather.5.cloned.1.call-update) | async-done | bytes 1572880 | tf_op jit(solution)/shard_map/all_gather | solution.py:53
  66.2 9.3 %convolution_convert_fusion = bf16[512,3072]{1,0:T(8,128)(2,1)} fusion(bf16[512,1536]{1,0:T(8,128)(2,1)} %all-gather.5.cloned.1.call-done, bf16[3072,1536]{1,0:T(8,128)(2,1)} %param.7), kind=kOutput, calls=%fused_computation.1 | convolution fusion | flops 4833411072 | bytes 14155776 | tf_op jit(solution)/shard_map/dot_general | solution.py:25
  75.5 0.0 reduce-scatter.7.cloned.1.call-update
  75.5 0.0 all-gather.7.cloned.1.call-start
  75.6 54.0 %reduce-scatter.5.cloned.1.call-done = bf16[128,3072]{1,0:T(8,128)(2,1)} async-done(((bf16[512,3072]{1,0:T(8,128)(2,1)}), bf16[128,3072]{1,0:T(8,128)(2,1)}) %reduce-scatter.5.cloned.1.call-update) | async-done | bytes 786448 | tf_op jit(solution)/shard_map/reduce_scatter | solution.py:55
  129.5 63.1 %reduce-scatter.7.cloned.1.call-done = bf16[128,3072]{1,0:T(8,128)(2,1)} async-done(((bf16[512,3072]{1,0:T(8,128)(2,1)}), bf16[128,3072]{1,0:T(8,128)(2,1)}) %reduce-scatter.7.cloned.1.call-update) | async-done | bytes 786448 | tf_op jit(solution)/shard_map/reduce_scatter | solution.py:59
  192.6 2.5 fusion.7
  195.2 1.3 pad_maximum_fusion
  196.4 0.0 all-gather.7.cloned.1.call-update
  196.4 0.0 reduce-scatter.9.cloned.1.call-start
  196.5 115.3 %all-gather.7.cloned.1.call-done = bf16[512,6144]{1,0:T(8,128)(2,1)} async-done(((bf16[128,6144]{1,0:T(8,128)(2,1)}), bf16[512,6144]{1,0:T(8,128)(2,1)}) %all-gather.7.cloned.1.call-update) | async-done | bytes 6291472 | tf_op jit(solution)/shard_map/all_gather | solution.py:65
  311.8 10.3 %convolution_convert_fusion.3 = bf16[512,1536]{1,0:T(8,128)(2,1)} fusion(bf16[3072,1536]{1,0:T(8,128)(2,1)} %param.7, bf16[512,6144]{1,0:T(8,128)(2,1)} %all-gather.7.cloned.1.call-done), kind=kOutput, calls=%fused_computation.11 | convolution fusion | flops 4832624640 | bytes 14155776 | tf_op jit(solution)/shard_map/dot_general | solution.py:71
  322.1 0.0 reduce-scatter.9.cloned.1.call-update
  322.1 0.2 reduce-scatter.11.cloned.1.call-start
  322.4 10.5 %convolution_convert_fusion.2 = bf16[512,1536]{1,0:T(8,128)(2,1)} fusion(bf16[1536,3072]{1,0:T(8,128)(2,1)} %param.6, bf16[512,6144]{1,0:T(8,128)(2,1)} %all-gather.7.cloned.1.call-done), kind=kOutput, calls=%fused_computation.10 | convolution fusion | flops 4832624640 | bytes 14155776 | tf_op jit(solution)/shard_map/dot_general | solution.py:25
  332.9 0.0 copy-start.2
  332.9 0.0 reduce-scatter.11.cloned.1.call-update
  332.9 1.4 copy-done.2
  334.3 11.4 %convolution_bitcast_fusion = f32[1536,3072]{0,1:T(8,128)} fusion(bf16[512,6144]{1,0:T(8,128)(2,1)} %all-gather.7.cloned.1.call-done, bf16[1,512,1536]{2,1,0:T(8,128)(2,1)S(1)} %copy-done.2), kind=kOutput, calls=%fused_computation | convolution fusion | flops 4831838208 | bytes 23592960 | tf_op jit(solution)/shard_map/dot_general | solution.py:31
  345.7 0.0 copy-start.3
  345.7 18.8 %copy.9 = f32[1536,3072]{1,0:T(8,128)} copy(f32[1536,3072]{0,1:T(8,128)} %convolution_bitcast_fusion) | data formatting | bytes 37748736
  364.5 0.0 copy-done.3
  364.5 0.0 copy-start
  364.5 0.0 copy-start.1
  364.5 11.5 %fusion.2 = f32[3072,1536]{1,0:T(8,128)} fusion(bf16[512,1536]{1,0:T(8,128)(2,1)S(1)} %copy-done.3, bf16[512,6144]{1,0:T(8,128)(2,1)} %all-gather.7.cloned.1.call-done), kind=kOutput, calls=%fused_computation.14 | convolution fusion | flops 4831838208 | bytes 23592960 | tf_op jit(solution)/shard_map/dot_general | solution.py:31
  376.0 0.0 reduce-scatter.9.cloned.1.call-done
  376.0 0.0 copy-done
  376.0 1.7 fusion.22
  377.7 22.9 %reduce-scatter.11.cloned.1.call-done = bf16[64,1536]{1,0:T(8,128)(2,1)} async-done(((bf16[512,1536]{1,0:T(8,128)(2,1)}), bf16[64,1536]{1,0:T(8,128)(2,1)}) %reduce-scatter.11.cloned.1.call-update) | async-done | bytes 196624 | tf_op jit(solution)/shard_map/reduce_scatter | solution.py:78
  400.5 0.0 copy-done.1
  400.5 1.7 fusion.21
Async XLA Ops:
  7.2 31.0 %all-gather.9.cloned.1.call-start = ((), (), s32[]{:S(2)}) async-start(), calls=%async_computation.10 | async-start | bytes 1769472 | tf_op jit(solution)/shard_map/all_gather | solution.py:52
  7.9 58.3 %all-gather.5.cloned.1.call-start = ((), (), s32[]{:S(2)}) async-start(), calls=%async_computation.5 | async-start | bytes 1769472 | tf_op jit(solution)/shard_map/all_gather | solution.py:53
  12.3 117.2 %reduce-scatter.5.cloned.1.call-start = ((), (), s32[]{:S(2)}) async-start(), calls=%async_computation.4 | async-start | bytes 3932160 | tf_op jit(solution)/shard_map/reduce_scatter | solution.py:55
  47.4 145.2 %reduce-scatter.7.cloned.1.call-start = ((), (), s32[]{:S(2)}) async-start(), calls=%async_computation.6 | async-start | bytes 3932160 | tf_op jit(solution)/shard_map/reduce_scatter | solution.py:59
  75.5 236.3 %all-gather.7.cloned.1.call-start = ((), (), s32[]{:S(2)}) async-start(), calls=%async_computation.7 | async-start | bytes 7864320 | tf_op jit(solution)/shard_map/all_gather | solution.py:65
  196.4 179.6 %reduce-scatter.9.cloned.1.call-start = ((), (), s32[]{:S(2)}) async-start(), calls=%async_computation.8 | async-start | bytes 1769472 | tf_op jit(solution)/shard_map/reduce_scatter | solution.py:72
  322.1 78.4 %reduce-scatter.11.cloned.1.call-start = ((), (), s32[]{:S(2)}) async-start(), calls=%async_computation.9 | async-start | bytes 1769472 | tf_op jit(solution)/shard_map/reduce_scatter | solution.py:78
  332.9 1.4 copy-start.2
  345.7 18.8 %copy-start.3 = (bf16[512,1536]{1,0:T(8,128)(2,1)S(1)}, bf16[512,1536]{1,0:T(8,128)(2,1)}, u32[]{:S(2)}) copy-start(bf16[512,1536]{1,0:T(8,128)(2,1)} %all-gather.5.cloned.1.call-done) | copy-start | bytes 4718596
  364.5 11.5 %copy-start = (bf16[1,64,1536]{2,1,0:T(8,128)(2,1)S(1)}, bf16[1,64,1536]{2,1,0:T(8,128)(2,1)}, u32[]{:S(2)}) copy-start(bf16[1,64,1536]{2,1,0:T(8,128)(2,1)} %param.5) | copy-start | bytes 589828
  364.5 36.0 %copy-start.1 = (bf16[1,64,1536]{2,1,0:T(8,128)(2,1)S(1)}, bf16[1,64,1536]{2,1,0:T(8,128)(2,1)}, u32[]{:S(2)}) copy-start(bf16[1,64,1536]{2,1,0:T(8,128)(2,1)} %param.8) | copy-start | bytes 589828
Sparse Core Ops, SparseCore 0:
  9.9 28.2 all-gather.8
  40.6 25.5 all-gather.4
  69.1 60.3 reduce-scatter.4
  132.3 60.3 reduce-scatter.6
  196.6 115.2 all-gather.6
  322.3 36.5 reduce-scatter.8
  362.1 38.3 reduce-scatter.10
